TPU v7x, 32 devices: a whole 2x2x4 slice. The times are simulated.
32 devices in a mesh: row: 8 (over y, x, core), col: 4 (over z).
Axes of the slice: x: 2, y: 2, z: 4, core: 2. Of those that a mesh axis runs over, the one named last changes fastest.
Arguments:
- layer_input: bfloat16 [256, 6144], P('row', 'col'), may hold values from -6 to 6
- norm_gain_rows: float32 [2, 6144], P(None, 'col'), may hold values from 0.1 to 1.9
- norm_bias_rows: float32 [2, 6144], P(None, 'col'), may hold values from -3 to 3
- query_key_value_weight: bfloat16 [6144, 3, 6144], P('col', None, 'row'), may hold values from -0.078125 to 0.078125
- adapter_down_maps: bfloat16 [64, 16, 6144], P(None, None, 'col'), may hold values from -0.078125 to 0.078125
- adapter_up_maps: bfloat16 [64, 16, 3, 6144], P(None, None, None, 'row'), may hold values from -6.5 to 6.5
- output_projection: bfloat16 [6144, 6144], P('row', 'col'), may hold values from -0.078125 to 0.078125
- up_projection: bfloat16 [6144, 24576], P('col', 'row'), may hold values from -0.078125 to 0.078125
- down_projection: bfloat16 [24576, 6144], P('row', 'col'), may hold values from -0.0390625 to 0.0390625
- prompt_token_length: int32 [4], replicated, may hold values from 1 to 64, 160 in all
- adapter_index: int32 [4], replicated, may hold values from 0 to 63
- prompt_page_map: int32 [4], replicated, may hold values from 0 to 3, each once
Outputs:
- new_hidden: bfloat16 [256, 6144], P('row', 'col')
- kv_pages: bfloat16 [4, 2, 64, 6144], P('col', None, None, 'row')
Inputs may be any that keep to these rules, and one draw needn't show every extreme that they name: `prompt_page_map`: each page is named by exactly one prompt. `prompt_token_length`: the prompts together hold 4 * 64 * 5 // 8 real tokens; some prompt fills all 64 positions.
All inputs are finite; a program needn't handle non-finite values.
Results may differ from a plain program's by a relative error of at most 0.023.
Values may be sent and summed in bfloat16 or wider, within the bound.
A program may use at most 128 MiB of HBM per device.

v0:
```python
import jax
import jax.numpy as jnp
from jax import lax
from jax.sharding import PartitionSpec as P

MODEL_WIDTH = 6144
HD = 96
ROT = 24


def normalize(hidden_f32, moments, gain_row, bias_row):
    row_mean = (moments[0] / MODEL_WIDTH)[:, None]
    row_var = (moments[1] / MODEL_WIDTH)[:, None] - row_mean * row_mean
    return ((hidden_f32 - row_mean) * lax.rsqrt(row_var + 1e-05) * gain_row + bias_row).astype(
        jnp.bfloat16
    )


def rotate(heads_in, positions):
    half_rot = ROT // 2
    inv_freq = 10000.0 ** (-jnp.arange(half_rot, dtype=jnp.float32) * 2.0 / ROT)
    angles = positions.astype(jnp.float32)[:, None] * inv_freq[None, :]
    cosine = jnp.cos(angles)[:, None, :]
    sine_part = jnp.sin(angles)[:, None, :]
    front_part = heads_in[..., :half_rot]
    back_part = heads_in[..., half_rot:ROT]
    return jnp.concatenate(
        [
            front_part * cosine - back_part * sine_part,
            back_part * cosine + front_part * sine_part,
            heads_in[..., ROT:],
        ],
        axis=-1,
    )


def per_device(
    layer_input,
    norm_gain_rows,
    norm_bias_rows,
    query_key_value_weight,
    adapter_down_maps,
    adapter_up_maps,
    output_projection,
    up_projection,
    down_projection,
    prompt_token_length,
    adapter_index,
    prompt_page_map,
):
    col_width = layer_input.shape[1]
    hidden_f32 = layer_input.astype(jnp.float32)
    moments = lax.psum(
        (jnp.sum(hidden_f32, axis=-1), jnp.sum(hidden_f32 * hidden_f32, axis=-1)), "col"
    )
    normed_attn = normalize(hidden_f32, moments, norm_gain_rows[0], norm_bias_rows[0])
    normed_mlp = normalize(hidden_f32, moments, norm_gain_rows[1], norm_bias_rows[1])
    normed_attn, normed_mlp = (
        lax.all_gather(normed_attn, "row", axis=0, tiled=True),
        lax.all_gather(normed_mlp, "row", axis=0, tiled=True),
    )
    col_count = lax.axis_size("col")
    prompt_span = normed_attn.shape[0] // col_count
    wide_weight = query_key_value_weight.reshape(col_width, -1)
    query_key_value_width = wide_weight.shape[1]
    adapter_wide_term = adapter_up_maps.reshape(
        adapter_up_maps.shape[0], adapter_up_maps.shape[1], query_key_value_width
    )
    slot_index = jnp.arange(col_count, dtype=jnp.int32)
    token_blocks = normed_attn.reshape(col_count, prompt_span, col_width)
    prompt = lax.axis_index("col")
    tok_slice = token_blocks.reshape(lax.axis_size("col") * prompt_span, col_width)
    base_term = jnp.dot(tok_slice, wide_weight, preferred_element_type=jnp.float32)
    selected_adapter = jnp.take(adapter_index, slot_index, axis=0)
    select_down = adapter_down_maps[selected_adapter]
    select_up = adapter_wide_term[selected_adapter]
    low_rank = jnp.einsum(
        "pld,prd->plr", token_blocks, select_down, preferred_element_type=jnp.float32
    ).astype(jnp.bfloat16)
    extra_term = jnp.einsum("plr,prk->plk", low_rank, select_up, preferred_element_type=jnp.float32)
    qkv_rows = lax.psum_scatter(
        (
            base_term
            + extra_term.reshape(lax.axis_size("col") * prompt_span, query_key_value_width)
        ).astype(jnp.bfloat16),
        "col",
        scatter_dimension=0,
        tiled=True,
    ).astype(jnp.float32)
    local_heads = query_key_value_width // (3 * HD)
    qkv_rows = qkv_rows.reshape(prompt_span, 3, local_heads, HD)
    positions = jnp.arange(prompt_span, dtype=jnp.int32)
    prompt_len = lax.dynamic_slice_in_dim(prompt_token_length, prompt, 1, 0)[0]
    live_mask = positions < prompt_len
    query = rotate(qkv_rows[:, 0], positions).astype(jnp.bfloat16)
    key_rows = rotate(qkv_rows[:, 1], positions).astype(jnp.bfloat16)
    value_rows = qkv_rows[:, 2].astype(jnp.bfloat16)
    zero_key = jnp.zeros_like(key_rows)
    key_rows = jnp.where(live_mask[:, None, None], key_rows, zero_key)
    value_rows = jnp.where(live_mask[:, None, None], value_rows, zero_key)
    scores = jnp.einsum(
        "qhe,khe->hqk", query, key_rows, preferred_element_type=jnp.float32
    ) / jnp.sqrt(jnp.float32(HD))
    allowed = (positions[None, :] <= positions[:, None]) & live_mask[None, :]
    scores = jnp.where(allowed[None, :, :], scores, jnp.float32(-1e30))
    top_score = jnp.max(scores, axis=-1, keepdims=True)
    expo = jnp.exp(scores - top_score)
    probs = (expo / jnp.sum(expo, axis=-1, keepdims=True)).astype(jnp.bfloat16)
    attended = jnp.einsum(
        "hqk,khe->qhe", probs, value_rows, preferred_element_type=jnp.float32
    ).astype(jnp.bfloat16)
    attended = attended.reshape(prompt_span, local_heads * HD)
    page_local = jnp.stack(
        [key_rows.reshape(prompt_span, -1), value_rows.reshape(prompt_span, -1)], axis=0
    )[None]
    target_hit = (prompt_page_map == prompt).astype(jnp.bfloat16)
    kv_pages = jnp.einsum(
        "p,pslk->slk",
        target_hit,
        lax.all_gather(page_local, "col", axis=0, tiled=True),
        preferred_element_type=jnp.float32,
    )[None].astype(jnp.bfloat16)
    tok_slice = normed_mlp
    up_rows = lax.psum_scatter(
        jnp.dot(tok_slice, up_projection, preferred_element_type=jnp.float32).astype(jnp.bfloat16),
        "col",
        scatter_dimension=0,
        tiled=True,
    ).astype(jnp.float32)
    hidden = jax.nn.gelu(up_rows, approximate=False).astype(jnp.bfloat16)
    attn_whole, hidden_whole = (
        lax.all_gather(attended, "col", axis=0, tiled=True),
        lax.all_gather(hidden, "col", axis=0, tiled=True),
    )
    branch = lax.psum_scatter(
        (
            jnp.dot(attn_whole, output_projection, preferred_element_type=jnp.float32)
            + jnp.dot(hidden_whole, down_projection, preferred_element_type=jnp.float32)
        ).astype(jnp.bfloat16),
        "row",
        scatter_dimension=0,
        tiled=True,
    ).astype(jnp.float32)
    new_hidden = (layer_input.astype(jnp.float32) + branch).astype(jnp.bfloat16)
    return (new_hidden, kv_pages)


def solution(mesh):
    return jax.shard_map(
        per_device,
        mesh=mesh,
        in_specs=(
            P("row", "col"),
            P(None, "col"),
            P(None, "col"),
            P("col", None, "row"),
            P(None, None, "col"),
            P(None, None, None, "row"),
            P("row", "col"),
            P("col", "row"),
            P("row", "col"),
            P(),
            P(),
            P(),
        ),
        out_specs=(P("row", "col"), P("col", None, None, "row")),
        check_vma=False,
    )
```

profile of v0, /device:TPU:0, one launch (start us, length us, event | category | flops | bytes accessed | tf_op | source)
XLA Modules:
  0.0 197.1 jit_solution(14919838215069900529)
XLA Ops:
  7.2 1.2 convert_reduce_fusion
  8.4 13.5 %all-reduce = (f32[32]{0:T(128)S(1)}, f32[32]{0:T(128)S(1)}) all-reduce(f32[32]{0:T(128)S(1)} %get-tuple-element.3, f32[32]{0:T(128)S(1)} %get-tuple-element.2), channel_id=1, replica_groups=mesh['row'=8,'col'=4] {'col'}, use_global_device_ids=true, to_apply=%region_3.0 | all-reduce | flops 64 | bytes 512 | tf_op jit(solution)/shard_map/psum | solution.py:53
  21.9 0.9 slice_reduce_fusion.2
  22.7 1.0 fusion.45
  23.8 10.4 %all_gather.17 = bf16[256,1536]{1,0:T(8,128)(2,1)S(1)} all-gather(bf16[32,1536]{1,0:T(8,128)(2,1)S(1)} %get-tuple-element.17), channel_id=1, replica_groups=mesh['row'=8,'col'=4] {'row'}, dimensions={0}, use_global_device_ids=true | all-gather | bytes 884736 | tf_op jit(solution)/shard_map/all_gather | solution.py:60
  34.2 7.4 %convolution_convert_fusion = bf16[256,3072]{1,0:T(8,128)(2,1)} fusion(bf16[256,1536]{1,0:T(8,128)(2,1)S(1)} %all_gather.17, bf16[1536,3072]{1,0:T(8,128)(2,1)} %param.19), kind=kOutput, calls=%fused_computation.6 | convolution fusion | flops 2416705536 | bytes 11796480 | tf_op jit(solution)/shard_map/dot_general | solution.py:125
  41.7 4.8 %copy.43 = bf16[64,3,2,8,768]{4,3,1,2,0:T(8,128)(2,1)} copy(bf16[64,3,2,8,768]{4,3,2,1,0:T(8,128)(2,1)} %bitcast.55) | data formatting | bytes 9437184 | tf_op jit(solution)/shard_map/reshape | solution.py:66
  46.5 0.6 gather_fusion
  47.1 2.9 %gather_fusion.2 = bf16[4,16,2304]{2,1,0:T(8,128)(2,1)S(1)} fusion(bf16[64,16,2304]{2,1,0:T(8,128)(2,1)} %bitcast.54, s32[1024]{0:T(1024)S(1)} %pad_clamp_fusion), kind=kCustom, calls=%fused_computation.2 | custom fusion | bytes 589840 | tf_op jit(solution)/shard_map/gather | solution.py:76
  50.0 1.2 gather_fusion.1
  51.3 10.3 %copy.27 = bf16[1536,3,768]{0,2,1:T(8,128)(2,1)} copy(bf16[1536,3,768]{2,0,1:T(8,128)(2,1)} %param.15) | data formatting | bytes 14155776 | tf_op args[3]
  61.6 10.4 %all_gather.15 = bf16[256,1536]{1,0:T(8,128)(2,1)S(1)} all-gather(bf16[32,1536]{1,0:T(8,128)(2,1)S(1)} %get-tuple-element.16), channel_id=1, replica_groups=mesh['row'=8,'col'=4] {'row'}, dimensions={0}, use_global_device_ids=true | all-gather | bytes 884736 | tf_op jit(solution)/shard_map/all_gather | solution.py:59
  72.0 1.7 fusion.7
  73.6 6.2 %fusion.1 = bf16[256,2304]{1,0:T(8,128)(2,1)} fusion(f32[256,2304]{1,0:T(8,128)S(1)} %bitcast.61, bf16[256,1536]{1,0:T(8,128)(2,1)S(1)} %all_gather.15, bf16[1536,2304]{0,1:T(8,128)(2,1)} %bitcast.53), kind=kOutput, calls=%fused_computation.5 | convolution fusion | flops 1813118976 | bytes 11403264 | tf_op jit(solution)/shard_map/dot_general | solution.py:73
  79.9 0.6 dynamic_slice.3
  80.5 3.4 %fusion.9 = bf16[64,3072]{1,0:T(8,128)(2,1)} fusion(bf16[64,3072]{1,0:T(8,128)(2,1)} %reduce-scatter.6.cloned.1.call-done), kind=kLoop, calls=%fused_computation.21 | loop fusion | flops 12976128 | bytes 786432 | tf_op jit(solution)/shard_map/convert_element_type | solution.py:130
  83.9 0.0 reduce-scatter.8.cloned.1.call-start
  84.0 0.7 iota_compare_fusion.1
  84.7 0.1 fusion.62
  84.7 0.2 multiply_cosine_fusion
  84.9 21.5 %reduce-scatter.4.cloned.1.call-done = bf16[64,2304]{1,0:T(8,128)(2,1)} async-done(((bf16[256,2304]{1,0:T(8,128)(2,1)}), bf16[64,2304]{1,0:T(8,128)(2,1)}) %reduce-scatter.4.cloned.1.call-update) | async-done | bytes 294928 | tf_op jit(solution)/shard_map/reduce_scatter | solution.py:81
  106.4 1.5 reshape.213
  108.0 0.1 copy.57
  108.1 0.1 slice.67
  108.2 0.1 copy.58
  108.2 0.1 slice.81
  108.3 0.1 multiply_subtract_fusion
  108.5 0.1 maximum_convert_fusion
  108.7 0.1 subtract_convert_fusion
  108.8 0.3 fusion.80
  109.1 0.3 fusion.4
  109.4 0.3 fusion.6
  109.7 0.1 copy.33
  109.8 0.1 reshape.211
  109.9 17.8 %all_gather.16 = bf16[256,768]{1,0:T(8,128)(2,1)S(1)} all-gather(bf16[64,768]{1,0:T(8,128)(2,1)S(1)} %reshape.211), channel_id=1, replica_groups=mesh['row'=8,'col'=4] {'col'}, dimensions={0}, use_global_device_ids=true | all-gather | bytes 491520 | tf_op jit(solution)/shard_map/all_gather | solution.py:132
  127.8 19.5 %all-gather.3.cloned.1.call-done = bf16[256,3072]{1,0:T(8,128)(2,1)} async-done(((bf16[64,3072]{1,0:T(8,128)(2,1)}), bf16[256,3072]{1,0:T(8,128)(2,1)}) %all-gather.3.cloned.1.call-update) | async-done | bytes 1572880 | tf_op jit(solution)/shard_map/all_gather | solution.py:133
  147.2 5.6 %fusion.86 = f32[256,1536]{1,0:T(8,128)S(1)} fusion(bf16[256,3072]{1,0:T(8,128)(2,1)} %all-gather.3.cloned.1.call-done, bf16[3072,1536]{1,0:T(8,128)(2,1)} %param.20), kind=kOutput, calls=%fused_computation.124 | convolution fusion | flops 2415919104 | bytes 12582912 | tf_op jit(solution)/shard_map/dot_general | solution.py:138
  152.9 1.7 fusion.2
  154.6 0.1 copy.34
  154.7 0.8 convert_element_type.121
  155.5 0.1 copy.35
  155.6 0.1 convert_element_type.122
  155.7 1.1 broadcast_select_fusion.1
  156.9 18.0 %all-gather = bf16[8,64,768]{2,1,0:T(8,128)(2,1)S(1)} all-gather(bf16[2,64,768]{2,1,0:T(8,128)(2,1)S(1)} %pad_maximum_fusion), channel_id=2, replica_groups=mesh['row'=8,'col'=4] {'col'}, dimensions={0}, use_global_device_ids=true | all-gather | bytes 983040 | tf_op jit(solution)/shard_map/all_gather | solution.py:120
  175.0 0.7 fusion.39
  175.7 0.7 copy.59
  176.4 12.7 %reduce-scatter.8.cloned.1.call-done = bf16[32,1536]{1,0:T(8,128)(2,1)} async-done(((bf16[256,1536]{1,0:T(8,128)(2,1)}), bf16[32,1536]{1,0:T(8,128)(2,1)}) %reduce-scatter.8.cloned.1.call-update) | async-done | bytes 98320 | tf_op jit(solution)/shard_map/reduce_scatter | solution.py:135
  189.1 1.6 fusion.49
  (33 shorter events, 0.4 us)
Async XLA Ops:
  7.2 42.9 %copy-start = (bf16[64,16,1536]{2,1,0:T(8,128)(2,1)S(1)}, bf16[64,16,1536]{2,1,0:T(8,128)(2,1)}, u32[]{:S(2)}) copy-start(bf16[64,16,1536]{2,1,0:T(8,128)(2,1)} %param.16) | copy-start | bytes 9437188
  7.2 73.3 %reduce-scatter.6.cloned.1.call-start = ((), (), s32[]{:S(2)}) async-start(), calls=%async_computation.4 | async-start | bytes 1966080 | tf_op jit(solution)/shard_map/reduce_scatter | solution.py:124
  41.6 64.8 %reduce-scatter.4.cloned.1.call-start = ((), (), s32[]{:S(2)}) async-start(), calls=%async_computation.3 | async-start | bytes 1474560 | tf_op jit(solution)/shard_map/reduce_scatter | solution.py:81
  41.7 4.8 %copy-start.2 = (s32[4]{0:T(128)S(1)}, s32[4]{0:T(128)}, u32[]{:S(2)}) copy-start(s32[4]{0:T(128)} %param.22) | copy-start | bytes 52
  73.6 6.3 %copy-start.5 = (s32[4]{0:T(128)S(1)}, s32[4]{0:T(128)}, u32[]{:S(2)}) copy-start(s32[4]{0:T(128)} %param.21) | copy-start | bytes 52
  79.8 67.4 %all-gather.3.cloned.1.call-start = ((), (), s32[]{:S(2)}) async-start(), calls=%async_computation.5 | async-start | bytes 1966080 | tf_op jit(solution)/shard_map/all_gather | solution.py:133
  83.9 105.1 %reduce-scatter.8.cloned.1.call-start = ((), (), s32[]{:S(2)}) async-start(), calls=%async_computation.6 | async-start | bytes 884736 | tf_op jit(solution)/shard_map/reduce_scatter | solution.py:135
  127.8 25.1 %copy-start.3 = (bf16[768,1536]{1,0:T(8,128)(2,1)S(1)}, bf16[768,1536]{1,0:T(8,128)(2,1)}, u32[]{:S(2)}) copy-start(bf16[768,1536]{1,0:T(8,128)(2,1)} %param.18) | copy-start | bytes 7077892
  154.6 20.4 %copy-start.6 = (s32[4]{0:T(128)S(1)}, s32[4]{0:T(128)}, u32[]{:S(2)}) copy-start(s32[4]{0:T(128)} %param.23) | copy-start | bytes 52
  155.5 33.5 %copy-start.4 = (bf16[32,1536]{1,0:T(8,128)(2,1)S(1)}, bf16[32,1536]{1,0:T(8,128)(2,1)}, u32[]{:S(2)}) copy-start(bf16[32,1536]{1,0:T(8,128)(2,1)} %param.12) | copy-start | bytes 294916
  155.5 35.1 %copy-start.1 = (bf16[64,16,1536]{2,1,0:T(8,128)(2,1)S(1)}, bf16[64,16,1536]{2,1,0:T(8,128)(2,1)}, u32[]{:S(2)}) copy-start(bf16[64,16,1536]{2,1,0:T(8,128)(2,1)} %param.16) | copy-start | bytes 9437188
Sparse Core Ops, SparseCore 0:
  41.7 32.5 reduce-scatter.5
  79.9 26.4 reduce-scatter.3
  108.0 39.1 all-gather.2
  154.7 34.2 reduce-scatter.7
where the time goes:
time: 198 us; the launch traced here: 197 us
  blocking collectives  70.1 us (35%)
  waiting for transfers between devices  53.7 us (27%)
  local copies, waits for them, and re-layouts  25.3 us (13%)
  matrix products  24.1 us (12%)
  between operations  14 us (7%)
  other arithmetic  9.75 us (5%)
    reduce_scatter x1, waiting for transfers between devices, per_device(): lax.psum_scatter((base_term + extra_term.reshape(lax.axis_size('col') * p...  21.5 us
    all_gather x1, waiting for transfers between devices, per_device(): lax.all_gather(hidden, 'col', axis=0, tiled=True)  19.5 us
    all_gather x1, blocking collectives, per_device(): lax.all_gather(page_local, 'col', axis=0, tiled=True)  18 us
    all_gather x1, blocking collectives, per_device(): lax.all_gather(attended, 'col', axis=0, tiled=True)  17.8 us
    psum x1, blocking collectives, per_device(): lax.psum((jnp.sum(hidden_f32, axis=-1), jnp.sum(hidden_f32 * hidden_f32,...  13.5 us
    reduce_scatter x1, waiting for transfers between devices, per_device(): lax.psum_scatter((jnp.dot(attn_whole, output_projection, preferred_elemen...  12.7 us
    unnamed x18, local copies, waits for them, and re-layouts  10.5 us
    all_gather x1, blocking collectives, per_device(): lax.all_gather(normed_mlp, 'row', axis=0, tiled=True)  10.4 us
  transfers between devices with their start and end apart: 4, of which 3 were waited for; matrix products, arithmetic and copies ran while one was open for 20% of the time, Pallas kernels for 0%

commit v1 on v0

--- a/solution.py
+++ b/solution.py
@@ -1,3 +1,4 @@
+import functools
 import jax
 import jax.numpy as jnp
 from jax import lax
@@ -6,6 +7,32 @@
 MODEL_WIDTH = 6144
 HD = 96
 ROT = 24
+
+
+def feed_rails(arr_in, dim_no):
+    y_new = list(arr_in.shape[1:])
+    y_new[dim_no] *= arr_in.shape[0]
+    return jnp.moveaxis(arr_in, 0, dim_no).reshape(y_new)
+
+
+def supply_all_ticks(z, chip_axis):
+    w_next, mat_out = (lax.axis_size(chip_axis), lax.axis_index(chip_axis))
+    response, plain = (z[None], 1)
+    while plain < w_next:
+        x_next = lax.ppermute(response, chip_axis, [(j0, j0 ^ plain) for j0 in range(w_next)])
+        found_now = mat_out & plain == 0
+        response = jnp.concatenate(
+            [jnp.where(found_now, response, x_next), jnp.where(found_now, x_next, response)]
+        )
+        plain *= 2
+    return response
+
+
+def inputs_edit(row_data, block_in, dim_i):
+    return feed_rails(supply_all_ticks(row_data, block_in), dim_i)
+
+
+detail_racks_up = functools.partial(inputs_edit, block_in="col", dim_i=0)
 
 
 def normalize(hidden_f32, moments, gain_row, bias_row):
@@ -129,7 +156,7 @@
     ).astype(jnp.float32)
     hidden = jax.nn.gelu(up_rows, approximate=False).astype(jnp.bfloat16)
     attn_whole, hidden_whole = (
-        lax.all_gather(attended, "col", axis=0, tiled=True),
+        detail_racks_up(attended),
         lax.all_gather(hidden, "col", axis=0, tiled=True),
     )
     branch = lax.psum_scatter(

time: 198 us -> 224 us (1.13)
  waiting for transfers between devices: 53.7 us -> 93.6 us
  blocking collectives: 70.1 us -> 53.2 us
    reduce_scatter x1, waiting for transfers between devices: 0.01 us -> 34.8 us  [per_device(): lax.psum_scatter(jnp.dot(tok_slice, up_projection, preferred_element_type...]
    ppermute x0 -> x2, waiting for transfers between devices: none -> 24.8 us  [supply_all_ticks(): lax.ppermute(response, chip_axis, [(j0, j0 ^ plain) for j0 in range(w_nex...]
    all_gather x1 -> x0, blocking collectives: 17.8 us -> none  [per_device(): lax.all_gather(attended, 'col', axis=0, tiled=True)]
    reduce_scatter x1, waiting for transfers between devices: 21.5 us -> 7.15 us  [per_device(): lax.psum_scatter((base_term + extra_term.reshape(lax.axis_size('col') * p...]
    all_gather x1, waiting for transfers between devices: 19.5 us -> 14 us  [per_device(): lax.all_gather(hidden, 'col', axis=0, tiled=True)]
  transfers between devices with their start and end apart: 4 -> 6, of which waited for: 3 -> 6; matrix products, arithmetic and copies ran while one was open for 20% -> 7% of each run, Pallas kernels for 0% -> 0%
where the time goes in v1:
time: 224 us; the launch traced here: 223 us
  waiting for transfers between devices  93.6 us (42%)
  blocking collectives  53.2 us (24%)
  local copies, waits for them, and re-layouts  26 us (12%)
  matrix products  24 us (11%)
  between operations  14 us (6%)
  other arithmetic  9.89 us (4%)
  starting transfers between devices  2.24 us (1%)
    reduce_scatter x1, waiting for transfers between devices, per_device(): lax.psum_scatter(jnp.dot(tok_slice, up_projection, preferred_element_type...  34.8 us
    ppermute x2, waiting for transfers between devices, supply_all_ticks(): lax.ppermute(response, chip_axis, [(j0, j0 ^ plain) for j0 in range(w_nex...  24.8 us
    all_gather x1, blocking collectives, per_device(): lax.all_gather(page_local, 'col', axis=0, tiled=True)  18 us
    all_gather x1, waiting for transfers between devices, per_device(): lax.all_gather(hidden, 'col', axis=0, tiled=True)  14 us
    psum x1, blocking collectives, per_device(): lax.psum((jnp.sum(hidden_f32, axis=-1), jnp.sum(hidden_f32 * hidden_f32,...  13.5 us
    reduce_scatter x1, waiting for transfers between devices, per_device(): lax.psum_scatter((jnp.dot(attn_whole, output_projection, preferred_elemen...  12.8 us
    all_gather x1, blocking collectives, per_device(): lax.all_gather(normed_attn, 'row', axis=0, tiled=True)  11.5 us
    unnamed x18, local copies, waits for them, and re-layouts  10.5 us
  transfers between devices with their start and end apart: 6, of which 6 were waited for; matrix products, arithmetic and copies ran while one was open for 7% of the time, Pallas kernels for 0%

profile of v1, /device:TPU:0, one launch (start us, length us, event | category | flops | bytes accessed | tf_op | source)
XLA Modules:
  0.0 223.0 jit_solution(9020402217835824067)
XLA Ops:
  7.2 1.2 convert_reduce_fusion
  8.4 13.5 %all-reduce = (f32[32]{0:T(128)S(1)}, f32[32]{0:T(128)S(1)}) all-reduce(f32[32]{0:T(128)S(1)} %get-tuple-element.3, f32[32]{0:T(128)S(1)} %get-tuple-element.2), channel_id=1, replica_groups=mesh['row'=8,'col'=4] {'col'}, use_global_device_ids=true, to_apply=%region_3.0 | all-reduce | flops 64 | bytes 512 | tf_op jit(solution)/shard_map/psum | solution.py:80
  21.9 0.9 slice_reduce_fusion.2
  22.7 1.0 fusion.45
  23.8 11.5 %all_gather.12 = bf16[256,1536]{1,0:T(8,128)(2,1)} all-gather(bf16[32,1536]{1,0:T(8,128)(2,1)S(1)} %get-tuple-element.20), channel_id=1, replica_groups=mesh['row'=8,'col'=4] {'row'}, dimensions={0}, use_global_device_ids=true | all-gather | bytes 884736 | tf_op jit(solution)/shard_map/all_gather | solution.py:86
  35.2 1.3 gather_fusion
  36.5 4.8 %copy.43 = bf16[64,3,2,8,768]{4,3,1,2,0:T(8,128)(2,1)} copy(bf16[64,3,2,8,768]{4,3,2,1,0:T(8,128)(2,1)} %bitcast.56) | data formatting | bytes 9437184 | tf_op jit(solution)/shard_map/reshape | solution.py:93
  41.3 2.9 %gather_fusion.2 = bf16[4,16,2304]{2,1,0:T(8,128)(2,1)S(1)} fusion(bf16[64,16,2304]{2,1,0:T(8,128)(2,1)} %bitcast.55, s32[1024]{0:T(1024)S(1)} %pad_clamp_fusion), kind=kCustom, calls=%fused_computation.2 | custom fusion | bytes 589840 | tf_op jit(solution)/shard_map/gather | solution.py:103
  44.2 1.2 gather_fusion.1
  45.5 10.3 %copy.27 = bf16[1536,3,768]{0,2,1:T(8,128)(2,1)} copy(bf16[1536,3,768]{2,0,1:T(8,128)(2,1)} %param.15) | data formatting | bytes 14155776 | tf_op args[3]
  55.8 1.6 fusion.7
  57.5 6.0 %fusion.1 = bf16[256,2304]{1,0:T(8,128)(2,1)} fusion(f32[256,2304]{1,0:T(8,128)S(1)} %bitcast.62, bf16[256,1536]{1,0:T(8,128)(2,1)S(1)} %copy-done.2, bf16[1536,2304]{0,1:T(8,128)(2,1)} %bitcast.54), kind=kOutput, calls=%fused_computation.5 | convolution fusion | flops 1813118976 | bytes 11403264 | tf_op jit(solution)/shard_map/dot_general | solution.py:100
  63.6 10.3 %all_gather.13 = bf16[256,1536]{1,0:T(8,128)(2,1)S(1)} all-gather(bf16[32,1536]{1,0:T(8,128)(2,1)S(1)} %get-tuple-element.21), channel_id=1, replica_groups=mesh['row'=8,'col'=4] {'row'}, dimensions={0}, use_global_device_ids=true | all-gather | bytes 884736 | tf_op jit(solution)/shard_map/all_gather | solution.py:87
  73.9 7.5 %convolution_convert_fusion = bf16[256,3072]{1,0:T(8,128)(2,1)} fusion(bf16[256,1536]{1,0:T(8,128)(2,1)S(1)} %all_gather.13, bf16[1536,3072]{1,0:T(8,128)(2,1)} %param.19), kind=kOutput, calls=%fused_computation.6 | convolution fusion | flops 2416705536 | bytes 11796480 | tf_op jit(solution)/shard_map/dot_general | solution.py:152
  81.4 0.6 dynamic_slice.3
  82.0 0.7 iota_compare_fusion.1
  82.8 0.2 multiply_cosine_fusion
  83.0 7.1 %reduce-scatter.4.cloned.1.call-done = bf16[64,2304]{1,0:T(8,128)(2,1)} async-done(((bf16[256,2304]{1,0:T(8,128)(2,1)}), bf16[64,2304]{1,0:T(8,128)(2,1)}) %reduce-scatter.4.cloned.1.call-update) | async-done | bytes 294928 | tf_op jit(solution)/shard_map/reduce_scatter | solution.py:108
  90.1 1.5 reshape.213
  91.7 34.8 %reduce-scatter.6.cloned.1.call-done = bf16[64,3072]{1,0:T(8,128)(2,1)} async-done(((bf16[256,3072]{1,0:T(8,128)(2,1)}), bf16[64,3072]{1,0:T(8,128)(2,1)}) %reduce-scatter.6.cloned.1.call-update) | async-done | bytes 393232 | tf_op jit(solution)/shard_map/reduce_scatter | solution.py:151
  126.5 3.5 %fusion.9 = bf16[64,3072]{1,0:T(8,128)(2,1)} fusion(bf16[64,3072]{1,0:T(8,128)(2,1)} %reduce-scatter.6.cloned.1.call-done), kind=kLoop, calls=%fused_computation.21 | loop fusion | flops 12976128 | bytes 786432 | tf_op jit(solution)/shard_map/convert_element_type | solution.py:157
  130.0 0.2 reduce-scatter.8.cloned.1.call-start
  130.3 0.1 slice.67
  130.5 0.1 slice.81
  130.6 0.1 multiply_subtract_fusion
  130.8 0.1 maximum_convert_fusion
  130.9 0.1 subtract_convert_fusion
  131.1 0.3 fusion.80
  131.4 0.3 fusion.4
  131.7 0.3 fusion.6
  131.9 0.1 copy.33
  132.0 0.1 broadcast_in_dim_reshape.3
  132.2 0.4 collective-permute-start
  132.6 4.2 %collective-permute-done = bf16[1,64,768]{2,1,0:T(8,128)(2,1)S(1)} collective-permute-done((bf16[1,64,768]{2,1,0:T(8,128)(2,1)S(1)}, bf16[1,64,768]{2,1,0:T(8,128)(2,1)S(1)}, u32[]{:S(2)}, u32[]{:S(2)}) %collective-permute-start) | collective-permute-done | bytes 98336 | tf_op jit(solution)/shard_map/ppermute | solution.py:22
  136.9 1.4 collective-permute-start.1
  138.4 20.6 %collective-permute-done.1 = bf16[2,64,768]{2,1,0:T(8,128)(2,1)S(1)} collective-permute-done((bf16[2,64,768]{2,1,0:T(8,128)(2,1)S(1)}, bf16[2,64,768]{2,1,0:T(8,128)(2,1)S(1)}, u32[]{:S(2)}, u32[]{:S(2)}) %collective-permute-start.1) | collective-permute-done | bytes 196640 | tf_op jit(solution)/shard_map/ppermute | solution.py:22
  159.0 14.0 %all-gather.3.cloned.1.call-done = bf16[256,3072]{1,0:T(8,128)(2,1)} async-done(((bf16[64,3072]{1,0:T(8,128)(2,1)}), bf16[256,3072]{1,0:T(8,128)(2,1)}) %all-gather.3.cloned.1.call-update) | async-done | bytes 1572880 | tf_op jit(solution)/shard_map/all_gather | solution.py:160
  173.0 5.6 %fusion.86 = f32[256,1536]{1,0:T(8,128)S(1)} fusion(bf16[256,3072]{1,0:T(8,128)(2,1)} %all-gather.3.cloned.1.call-done, bf16[3072,1536]{1,0:T(8,128)(2,1)} %param.20), kind=kOutput, calls=%fused_computation.130 | convolution fusion | flops 2415919104 | bytes 12582912 | tf_op jit(solution)/shard_map/dot_general | solution.py:165
  178.6 1.7 fusion.2
  180.3 0.1 copy.34
  180.5 0.8 convert_element_type.121
  181.4 0.1 convert_element_type.122
  181.5 1.1 broadcast_select_fusion.3
  182.7 18.0 %all-gather = bf16[8,64,768]{2,1,0:T(8,128)(2,1)S(1)} all-gather(bf16[2,64,768]{2,1,0:T(8,128)(2,1)S(1)} %pad_maximum_fusion.2), channel_id=2, replica_groups=mesh['row'=8,'col'=4] {'col'}, dimensions={0}, use_global_device_ids=true | all-gather | bytes 983040 | tf_op jit(solution)/shard_map/all_gather | solution.py:147
  200.7 0.7 fusion.39
  201.4 0.7 copy.59
  202.1 12.8 %reduce-scatter.8.cloned.1.call-done = bf16[32,1536]{1,0:T(8,128)(2,1)} async-done(((bf16[256,1536]{1,0:T(8,128)(2,1)}), bf16[32,1536]{1,0:T(8,128)(2,1)}) %reduce-scatter.8.cloned.1.call-update) | async-done | bytes 98320 | tf_op jit(solution)/shard_map/reduce_scatter | solution.py:162
  214.9 1.6 fusion.49
  (40 shorter events, 0.8 us)
Async XLA Ops:
  7.2 37.1 %copy-start = (bf16[64,16,1536]{2,1,0:T(8,128)(2,1)S(1)}, bf16[64,16,1536]{2,1,0:T(8,128)(2,1)}, u32[]{:S(2)}) copy-start(bf16[64,16,1536]{2,1,0:T(8,128)(2,1)} %param.16) | copy-start | bytes 9437188
  7.2 83.0 %reduce-scatter.4.cloned.1.call-start = ((), (), s32[]{:S(2)}) async-start(), calls=%async_computation.3 | async-start | bytes 1474560 | tf_op jit(solution)/shard_map/reduce_scatter | solution.py:108
  45.5 10.4 %copy-start.2 = (bf16[256,1536]{1,0:T(8,128)(2,1)S(1)}, bf16[256,1536]{1,0:T(8,128)(2,1)}, u32[]{:S(2)}) copy-start(bf16[256,1536]{1,0:T(8,128)(2,1)} %all_gather.12) | copy-start | bytes 2359300
  63.5 63.0 %reduce-scatter.6.cloned.1.call-start = ((), (), s32[]{:S(2)}) async-start(), calls=%async_computation.4 | async-start | bytes 1966080 | tf_op jit(solution)/shard_map/reduce_scatter | solution.py:151
  73.9 7.5 %copy-start.5 = (s32[4]{0:T(128)S(1)}, s32[4]{0:T(128)}, u32[]{:S(2)}) copy-start(s32[4]{0:T(128)} %param.21) | copy-start | bytes 52
  81.4 91.6 %all-gather.3.cloned.1.call-start = ((), (), s32[]{:S(2)}) async-start(), calls=%async_computation.5 | async-start | bytes 1966080 | tf_op jit(solution)/shard_map/all_gather | solution.py:160
  130.0 84.9 %reduce-scatter.8.cloned.1.call-start = ((), (), s32[]{:S(2)}) async-start(), calls=%async_computation.6 | async-start | bytes 884736 | tf_op jit(solution)/shard_map/reduce_scatter | solution.py:162
  132.2 4.7 %collective-permute-start = (bf16[1,64,768]{2,1,0:T(8,128)(2,1)S(1)}, bf16[1,64,768]{2,1,0:T(8,128)(2,1)S(1)}, u32[]{:S(2)}, u32[]{:S(2)}) collective-permute-start(bf16[1,64,768]{2,1,0:T(8,128)(2,1)S(1)} %broadcast_in_dim_reshape.3), channel_id=1, source_target_pairs={{0,1},{1,0},{2,3},{3,2},{4,5},{5,4},{6,7},{7,6},{8,9},{9,8},{10,11... | collective-permute-start | bytes 294920 | tf_op jit(solution)/shard_map/ppermute | solution.py:22
  136.9 22.0 %collective-permute-start.1 = (bf16[2,64,768]{2,1,0:T(8,128)(2,1)S(1)}, bf16[2,64,768]{2,1,0:T(8,128)(2,1)S(1)}, u32[]{:S(2)}, u32[]{:S(2)}) collective-permute-start(bf16[2,64,768]{2,1,0:T(8,128)(2,1)S(1)} %pad_maximum_fusion.1), channel_id=1, source_target_pairs={{0,2},{1,3},{2,0},{3,1},{4,6},{5,7},{6,4},{7,5},{8,10},{9,11},{10,... | collective-permute-start | bytes 589832 | tf_op jit(solution)/shard_map/ppermute | solution.py:22
  159.0 19.6 %copy-start.3 = (bf16[768,1536]{1,0:T(8,128)(2,1)S(1)}, bf16[768,1536]{1,0:T(8,128)(2,1)}, u32[]{:S(2)}) copy-start(bf16[768,1536]{1,0:T(8,128)(2,1)} %param.18) | copy-start | bytes 7077892
  180.3 20.4 %copy-start.6 = (s32[4]{0:T(128)S(1)}, s32[4]{0:T(128)}, u32[]{:S(2)}) copy-start(s32[4]{0:T(128)} %param.23) | copy-start | bytes 52
  181.3 33.6 %copy-start.4 = (bf16[32,1536]{1,0:T(8,128)(2,1)S(1)}, bf16[32,1536]{1,0:T(8,128)(2,1)}, u32[]{:S(2)}) copy-start(bf16[32,1536]{1,0:T(8,128)(2,1)} %param.12) | copy-start | bytes 294916
  181.3 35.2 %copy-start.1 = (bf16[64,16,1536]{2,1,0:T(8,128)(2,1)S(1)}, bf16[64,16,1536]{2,1,0:T(8,128)(2,1)}, u32[]{:S(2)}) copy-start(bf16[64,16,1536]{2,1,0:T(8,128)(2,1)} %param.16) | copy-start | bytes 9437188
Sparse Core Ops, SparseCore 0:
  63.7 26.4 reduce-scatter.3
  92.4 34.0 reduce-scatter.5
  130.1 42.8 all-gather.2
  180.5 34.3 reduce-scatter.7
